TPU v7x, 256 devices: a whole 4x4x8 slice. The times are simulated.
256 devices in a mesh: row: 16 (over z, core), col: 16 (over y, x).
Axes of the slice: x: 4, y: 4, z: 8, core: 2. Of those that a mesh axis runs over, the one named last changes fastest.
Arguments:
- points: float32 [32, 65536], P(None, ('row', 'col')), may hold values from -6 to 6
- search: float32 [96, 65536], P(None, ('row', 'col')), may hold values from -24 to 24
Outputs:
- applied: float32 [96, 65536], P(None, ('row', 'col'))
- gram_a: float32 [96, 96], replicated
- gram_b: float32 [96, 96], replicated
- q_block: float32 [32, 65536], P(None, ('row', 'col'))
All inputs are finite; a program needn't handle non-finite values.
Results may differ from a plain program's by a relative error of at most 0.00036.
Values may be sent and summed in bfloat16 or wider, within the bound.
A program may use at most 128 MiB of HBM per device.

v0:
```python
import jax
import jax.numpy as jnp
from jax import lax
from jax.sharding import PartitionSpec as P

NEV = 32


def step_width():
    return 256


def pair_tile(source_points, source_squares, target_points, target_squares, kernel_rate):
    cross_terms = lax.dot_general(
        source_points,
        target_points,
        (((0,), (0,)), ((), ())),
        precision=lax.Precision.HIGHEST,
        preferred_element_type=jnp.float32,
    )
    return jnp.exp(
        -kernel_rate * (source_squares[:, None] + target_squares[None, :] - 2.0 * cross_terms)
    )


def degree_stored(source_points, source_squares, target_points, target_squares, kernel_rate):
    span_width = source_points.shape[1]
    stride = step_width()

    def degree_add_block(step_index, carry):
        running, stored = carry
        offset = step_index * stride
        block_points = lax.dynamic_slice_in_dim(source_points, offset, stride, 1)
        block_squares = lax.dynamic_slice_in_dim(source_squares, offset, stride, 0)
        affinity = pair_tile(
            block_points, block_squares, target_points, target_squares, kernel_rate
        )
        stored = lax.dynamic_update_slice_in_dim(stored, affinity.astype(jnp.bfloat16), offset, 0)
        return (running + jnp.sum(affinity, axis=0), stored)

    zero_sums = jnp.zeros((target_points.shape[1],), jnp.float32)
    empty_tile = jnp.zeros((span_width, target_points.shape[1]), jnp.bfloat16)
    return lax.fori_loop(0, span_width // stride, degree_add_block, (zero_sums, empty_tile))


def fold_stored(stored):

    def accumulate(running, shard_piece, first_index):
        span_width = shard_piece.shape[1]
        stride = step_width()

        def accumulate_add_block(step_index, partial_value):
            offset = step_index * stride
            columns = lax.dynamic_slice_in_dim(shard_piece, offset, stride, 1)
            tile_rows = lax.dynamic_slice_in_dim(stored, offset, stride, 0)
            return partial_value + jnp.dot(columns, tile_rows, preferred_element_type=jnp.float32)

        return lax.fori_loop(0, span_width // stride, accumulate_add_block, running)

    return accumulate


def degrees_and_fold(source_points, target_points, kernel_rate):
    target_squares = jnp.sum(target_points * target_points, axis=0)
    source_squares = jnp.sum(source_points * source_points, axis=0)
    partial_value, stored = degree_stored(
        source_points, source_squares, target_points, target_squares, kernel_rate
    )
    accumulate = fold_stored(stored)
    return (partial_value, accumulate)


def per_device(points, search):
    kernel_rate = 2.0 / points.shape[0]
    target_points = lax.all_gather(points, "col", axis=1, tiled=True)
    source_points = lax.all_gather(points, "row", axis=1, tiled=True)
    partial_value, accumulate = degrees_and_fold(source_points, target_points, kernel_rate)
    degrees = lax.psum_scatter(partial_value, "col", scatter_dimension=0, tiled=True)
    inverse_root = lax.rsqrt(degrees)
    scaled = (search * inverse_root[None, :]).astype(jnp.bfloat16)
    zero_sums = jnp.zeros((search.shape[0], target_points.shape[1]), jnp.float32)
    totals = accumulate(zero_sums, lax.all_gather(scaled, "row", axis=1, tiled=True), jnp.int32(0))
    applied = (
        lax.psum_scatter(totals, "col", scatter_dimension=1, tiled=True) * inverse_root[None, :]
    )
    point_count = search.shape[1] * lax.axis_size("row") * lax.axis_size("col")
    contract = (((1,), (1,)), ((), ()))
    local_a = lax.dot_general(
        search,
        applied,
        contract,
        precision=lax.Precision.HIGHEST,
        preferred_element_type=jnp.float32,
    )
    local_b = lax.dot_general(
        search,
        search,
        contract,
        precision=lax.Precision.HIGHEST,
        preferred_element_type=jnp.float32,
    )
    sum_a, sum_b = lax.psum((local_a, local_b), ("row", "col"))
    gram_a = sum_a / point_count
    gram_b = sum_b / point_count
    factor_b = jnp.linalg.cholesky(gram_b[:NEV, :NEV])
    mapping = jax.scipy.linalg.cho_solve((factor_b, True), gram_a[:NEV, :NEV]).T
    residual = applied[:NEV] - jnp.dot(mapping, search[:NEV], precision=lax.Precision.HIGHEST)
    local_r = lax.dot_general(
        residual,
        residual,
        contract,
        precision=lax.Precision.HIGHEST,
        preferred_element_type=jnp.float32,
    )
    residual_gram = lax.psum(local_r, ("row", "col")) / point_count
    factor_r = jnp.linalg.cholesky(residual_gram)
    q_block = jax.scipy.linalg.solve_triangular(factor_r, residual, lower=True)
    return (applied, gram_a, gram_b, q_block)


def solution(mesh):
    placed = (P(None, ("row", "col")), P(None, ("row", "col")))
    return jax.shard_map(
        per_device,
        mesh=mesh,
        in_specs=placed,
        out_specs=(P(None, ("row", "col")), P(), P(), P(None, ("row", "col"))),
        check_vma=False,
    )
```

profile of v0, /device:TPU:1, one launch (start us, length us, event | category | flops | bytes accessed | tf_op | source)
XLA Modules:
  0.0 711.1 jit_solution(5972083221102079643)
XLA Ops:
  7.2 20.0 %all_gather.10 = f32[32,4096]{1,0:T(8,128)S(1)} all-gather(f32[32,256]{1,0:T(8,128)} %param.7), channel_id=1, replica_groups=mesh['row'=16,'col'=16] {'col'}, dimensions={1}, use_global_device_ids=true | all-gather | bytes 557056 | tf_op jit(solution)/shard_map/all_gather | solution.py:75
  27.2 27.3 %all_gather.9 = f32[32,4096]{1,0:T(8,128)S(1)} all-gather(f32[32,256]{1,0:T(8,128)} %param.7), channel_id=1, replica_groups=mesh['row'=16,'col'=16] {'row'}, dimensions={1}, use_global_device_ids=true | all-gather | bytes 557056 | tf_op jit(solution)/shard_map/all_gather | solution.py:76
  54.6 11.0 %broadcast_in_dim.20 = bf16[4096,4096]{1,0:T(8,128)(2,1)} broadcast(bf16[]{:T(256)} %constant.130.clone.1), dimensions={} | broadcast | bytes 33554432 | tf_op jit(solution)/shard_map/broadcast_in_dim | solution.py:42
  65.6 98.8 %while.30 = (s32[]{:T(128)}, f32[4096]{0:T(1024)S(1)}, bf16[4096,4096]{1,0:T(8,128)(2,1)}, f32[4096]{0:T(1024)S(1)}, f32[4096]{0:T(1024)S(1)}, /*index=5*/f32[32...) while((s32[]{:T(128)}, f32[4096]{0:T(1024)S(1)}, ...), condition=%wide.region_4.0_spmd.clone, body=%wide.region_2.0_spmd.clone.sunk | while | flops 408948736 | bytes 6933681 | solution.py:43
  65.6 4.6 fusion.40
  71.8 4.6 fusion.40
  78.0 4.6 fusion.40
  84.1 4.6 fusion.40
  90.3 4.6 fusion.40
  96.5 4.6 fusion.40
  102.7 4.6 fusion.40
  108.9 4.6 fusion.40
  115.0 4.6 fusion.40
  121.2 4.6 fusion.40
  127.4 4.6 fusion.40
  133.5 4.6 fusion.40
  139.7 4.6 fusion.40
  145.9 4.6 fusion.40
  152.1 4.6 fusion.40
  158.3 4.6 fusion.40
  164.3 58.1 %all-reduce = f32[4096]{0:T(1024)S(1)} all-reduce(f32[4096]{0:T(1024)S(1)} %get-tuple-element.209), channel_id=2, replica_groups=mesh['row'=16,'col'=16] {'col'}, use_global_device_ids=true, to_apply=%region_5.0.clone | all-reduce | flops 4096 | bytes 32768
  223.8 30.7 %all_gather.11 = bf16[96,4096]{1,0:T(8,128)(2,1)S(1)} all-gather(bf16[96,256]{1,0:T(8,128)(2,1)S(1)} %multiply_convert_fusion), channel_id=1, replica_groups=mesh['row'=16,'col'=16] {'row'}, dimensions={1}, use_global_device_ids=true | all-gather | bytes 835584 | tf_op jit(solution)/shard_map/all_gather | solution.py:82
  254.5 38.2 %while.31 = (s32[]{:T(128)}, f32[96,4096]{1,0:T(8,128)S(1)}, bf16[96,4096]{1,0:T(8,128)(2,1)S(1)}, bf16[4096,4096]{1,0:T(8,128)(2,1)}, s32[]{:T(128)}, /*index=5*/s32[]{:T(128)}, s32[]{:T(128)}, s32[]{:T(128)}) while((s32[]{:T(128)}, f32[96,4096]{1,0:T(8,128)S(1)}, bf16[96,4096]{1,0:T(8,128)(2,1)S(1)}, ...), condition=%wide.region_7.0_spmd.clone, body=%wide.region_6.0_spmd.clone.sunk | while | flops 202113024 | bytes 5293708 | solution.py:58
  259.3 2.4 convolution_add_fusion.2
  261.7 2.4 convolution_add_fusion.2
  294.8 69.3 %reduce-scatter.2.cloned.1.call-done = f32[96,256]{1,0:T(8,128)} async-done(((f32[96,4096]{1,0:T(8,128)}), f32[96,256]{1,0:T(8,128)}) %reduce-scatter.2.cloned.1.call-update) | async-done | bytes 98320 | tf_op jit(solution)/shard_map/reduce_scatter | solution.py:84
  365.9 246.6 %all-reduce.4.cloned.1.call-done = (f32[96,96]{0,1:T(8,128)}, f32[96,96]{0,1:T(8,128)}) async-done(((f32[96,96]{0,1:T(8,128)}, f32[96,96]{0,1:T(8,128)}), (f32[96,96]{0,1:T(8,128)}, f32[96,96]{0,1:T(8,128)})) %all-reduce.4.cloned.1.call-update) | async-done | bytes 73744 | tf_op jit(solution)/shard_map/psum | solution.py:102
  614.1 2.9 cholesky.44
  618.4 2.4 custom-call.13
  622.3 74.3 %psum.23 = f32[32,32]{0,1:T(8,128)S(1)} all-reduce(f32[32,32]{0,1:T(8,128)S(1)} %fusion.24), channel_id=1, replica_groups=mesh['row'=16,'col'=16] {'row','col'}, use_global_device_ids=true, to_apply=%region_13.15 | all-reduce | flops 1024 | bytes 8192 | tf_op jit(solution)/shard_map/psum | solution.py:115
  696.7 2.9 cholesky.55
  701.0 2.4 custom-call.14
  (104 shorter events, 69.3 us)
Async XLA Ops:
  7.2 356.9 %reduce-scatter.2.cloned.1.call-start = ((), (), s32[]{:S(2)}) async-start(), calls=%async_computation.1 | async-start | bytes 1671168 | tf_op jit(solution)/shard_map/reduce_scatter | solution.py:84
  65.6 156.9 %copy-start.3 = (u32[256]{0:T(256)S(1)}, u32[256]{0:T(256)}, u32[]{:S(2)}) copy-start(u32[256]{0:T(256)} %constant.134) | copy-start | bytes 3076
  65.6 158.2 %copy-start.1 = (f32[96,256]{1,0:T(8,128)S(1)}, f32[96,256]{1,0:T(8,128)}, u32[]{:S(2)}) copy-start(f32[96,256]{1,0:T(8,128)} %param.8) | copy-start | bytes 294916
  292.7 1.2 copy-start
  293.9 318.6 %all-reduce.4.cloned.1.call-start = ((), (), s32[]{:S(2)}) async-start(), calls=%async_computation.2 | async-start | bytes 196608 | tf_op jit(solution)/shard_map/psum | solution.py:102
  365.0 339.3 %copy-start.2 = (f32[96,256]{1,0:T(8,128)}, f32[96,256]{1,0:T(8,128)S(1)}, u32[]{:S(2)}) copy-start(f32[96,256]{1,0:T(8,128)S(1)} %broadcast_multiply_fusion) | copy-start | bytes 294916
Sparse Core Ops, SparseCore 0:
  294.0 70.0 reduce-scatter.1
  370.3 242.1 all-reduce.3
where the time goes:
time: 712 us; the launch traced here: 711 us
  waiting for transfers between devices  316 us (44%)
  blocking collectives  210 us (29%)
  matrix products  115 us (16%)
  local copies, waits for them, and re-layouts  39.2 us (6%)
  other arithmetic  15.3 us (2%)
  between operations  14.8 us (2%)
    psum x1, waiting for transfers between devices, per_device(): sum_a, sum_b = lax.psum((local_a, local_b), ('row', 'col'))  247 us
    psum x1, blocking collectives, per_device(): residual_gram = lax.psum(local_r, ('row', 'col')) / point_count  74.3 us
    dot_general x16, matrix products, pair_tile(): lax.dot_general(source_points, target_points, (((0,), (0,)), ((), ())), p...  73.7 us
    reduce_scatter x1, waiting for transfers between devices, per_device(): lax.psum_scatter(totals, 'col', scatter_dimension=1, tiled=True)  69.3 us
    unnamed x1, blocking collectives  58.1 us
    dot_general x16, matrix products, accumulate_add_block(): jnp.dot(columns, tile_rows, preferred_element_type=jnp.float32)  37.7 us
    all_gather x1, blocking collectives, per_device(): lax.all_gather(scaled, 'row', axis=1, tiled=True)  30.7 us
    all_gather x1, blocking collectives, per_device(): source_points = lax.all_gather(points, 'row', axis=1, tiled=True)  27.3 us
  transfers between devices with their start and end apart: 2, of which 2 were waited for; matrix products, arithmetic and copies ran while one was open for 0% of the time, Pallas kernels for 0%

commit v1 on v0

v1 whole, which is shorter than its diff:
```python
import functools
import math

import jax
import jax.numpy as jnp
from jax import lax
from jax.experimental import pallas as pl
from jax.experimental.pallas import tpu as pltpu
from jax.sharding import PartitionSpec as P

NEV = 32
MESH = pl.DeviceIdType.MESH
HIGH = lax.Precision.HIGHEST
DEPTH = 256
LANES = 128


def contract(a, b, dims):
    return lax.dot_general(
        a, b, (dims, ((), ())), precision=HIGH, preferred_element_type=jnp.float32
    )


def split3(x):
    hi = x.astype(jnp.bfloat16)
    rest = x - hi.astype(jnp.float32)
    mid = rest.astype(jnp.bfloat16)
    low = (rest - mid.astype(jnp.float32)).astype(jnp.bfloat16)
    return hi, mid, low


def lifted(x, rate, is_source):
    dim, n = x.shape
    squares = jnp.broadcast_to(-rate * jnp.sum(x * x, axis=0, keepdims=True), (16, n))
    row = lax.broadcasted_iota(jnp.int32, (16, n), 0)
    parts = split3(squares)
    one = jnp.ones((16, n), jnp.float32)
    first = jnp.where(row == 0, parts[0].astype(jnp.float32), 0.0)
    first = jnp.where(row == 1, parts[1].astype(jnp.float32), first)
    first = jnp.where(row == 2, parts[2].astype(jnp.float32), first)
    second = jnp.where(row < 3, one, 0.0)
    if is_source:
        hi, mid, low = split3(x)
        blocks = [hi, hi, mid, hi, low, mid]
        extra = [first, second]
    else:
        hi, mid, low = split3(x * (2.0 * rate))
        blocks = [hi, mid, hi, low, hi, mid]
        extra = [second, first]
    blocks = blocks + [e.astype(jnp.bfloat16) for e in extra]
    used = 6 * dim + 32
    if used < DEPTH:
        blocks.append(jnp.zeros((DEPTH - used, n), jnp.bfloat16))
    return jnp.concatenate(blocks, axis=0)


def inverse_factor(gram):
    k = gram.shape[0]
    row = lax.broadcasted_iota(jnp.int32, (k, k), 0)
    col = lax.broadcasted_iota(jnp.int32, (k, k), 1)
    eye = jnp.where(row == col, 1.0, 0.0)
    pad = jnp.zeros((k, LANES - 2 * k), jnp.float32)
    work = jnp.concatenate([gram, eye, pad], axis=1)
    below = lax.broadcasted_iota(jnp.int32, (k, 1), 0)
    for step in range(k):
        pivot_row = work[step : step + 1, :]
        pivot = work[step : step + 1, step : step + 1]
        factor = jnp.where(below > step, work[:, step : step + 1] / pivot, 0.0)
        work = work - factor * pivot_row
    diagonal = jnp.sum(work[:, :k] * eye, axis=1, keepdims=True)
    return work[:, k : 2 * k] * lax.rsqrt(diagonal)


def pack(square):
    return jnp.concatenate([square[8 * i : 8 * i + 8, :] for i in range(4)], axis=1)


def unpack(flat):
    return jnp.concatenate([flat[:, 32 * i : 32 * i + 32] for i in range(4)], axis=0)


def kernel(
    R, C, n, points_ref, search_ref, applied_ref, gram_a_ref, gram_b_ref, q_ref,
    src_pts, tgt_pts, tgt_lift, tile, deg, deg_in, scal, outp, out_in,
    a_part, a_in, a_piece, a_in2, a_res,
    b_part, b_in, b_piece, b_in2, b_res,
    x_part, x_in, x_piece, x_in2,
    y_part, y_in, y_piece, y_in2,
    ssem, rsem,
):
    r = lax.axis_index("row")
    c = lax.axis_index("col")
    total = R * C * n
    rate = (2.0 / points_ref.shape[0]) * math.log2(math.e)
    Z = R // 2

    def along_row(d):
        return lax.rem(r + d, R)

    def along_col(d):
        return lax.rem(c + d, C)

    def row_copy(phase, src, dst, peer, slot):
        return pltpu.make_async_remote_copy(
            src_ref=src, dst_ref=dst, send_sem=ssem.at[phase, peer], recv_sem=rsem.at[phase, slot],
            device_id=(peer, c), device_id_type=MESH,
        )

    def col_copy(phase, src, dst, peer, slot):
        return pltpu.make_async_remote_copy(
            src_ref=src, dst_ref=dst, send_sem=ssem.at[phase, peer], recv_sem=rsem.at[phase, slot],
            device_id=(r, peer), device_id_type=MESH,
        )

    def row_all(phase, src_of, dst, what):
        def body(d, _):
            peer = along_row(d)
            if what == "start":
                row_copy(phase, src_of(peer), dst.at[r], peer, r).start()
            elif what == "recv":
                row_copy(phase, src_of(peer), dst.at[peer], peer, peer).wait_recv()
            else:
                row_copy(phase, src_of(peer), dst.at[r], peer, r).wait_send()
            return 0

        lax.fori_loop(1, R, body, 0)

    def col_all(phase, src_of, dst, what):
        def body(d, _):
            peer = along_col(d)
            if what == "start":
                col_copy(phase, src_of(peer), dst.at[c], peer, c).start()
            elif what == "recv":
                col_copy(phase, src_of(peer), dst.at[peer], peer, peer).wait_recv()
            else:
                col_copy(phase, src_of(peer), dst.at[c], peer, c).wait_send()
            return 0

        lax.fori_loop(1, C, body, 0)

    barrier = pltpu.get_barrier_semaphore()

    def greet_row(d, _):
        pl.semaphore_signal(barrier, inc=1, device_id=(along_row(d), c), device_id_type=MESH)
        return 0

    def greet_col(d, _):
        pl.semaphore_signal(barrier, inc=1, device_id=(r, along_col(d)), device_id_type=MESH)
        return 0

    lax.fori_loop(1, R, greet_row, 0)
    lax.fori_loop(1, C, greet_col, 0)
    pl.semaphore_wait(barrier, R + C - 2)

    TGT, SRC, DEG, SCAL, OUT, B1, B2, B3, A1, A2, A3, X1, X2, Y1, Y2 = range(15)
    my_points = lambda peer: points_ref
    col_all(TGT, my_points, tgt_pts, "start")
    row_all(SRC, my_points, src_pts, "start")
    src_pts[r] = points_ref[...]
    tgt_pts[c] = points_ref[...]

    rows = 96
    piece = LANES // R

    def stage_square(part, square):
        wide = jnp.concatenate([square, jnp.zeros((rows, LANES - rows), jnp.float32)], axis=1)
        for i in range(R):
            if (i + 1) * piece <= rows:
                part[i] = wide[i * piece : (i + 1) * piece]
            else:
                live = max(0, rows - i * piece)
                rest = jnp.zeros((piece - live, LANES), jnp.float32)
                part[i] = jnp.concatenate([wide[i * piece : i * piece + live], rest], axis=0) if live else rest

    def round1(phase, part, inbox):
        row_all(phase, lambda peer: part.at[peer], inbox, "start")
        inbox[r] = part[r]

    def round2(phase, part, inbox, piece_ref, inbox2):
        row_all(phase, lambda peer: part.at[peer], inbox, "recv")
        value = inbox[0]
        for i in range(1, R):
            value = value + inbox[i]
        piece_ref[0] = value
        col_all(phase + 1, lambda peer: piece_ref.at[0], inbox2, "start")
        inbox2[c] = value

    def round3(phase, piece_ref, inbox2, result):
        col_all(phase + 1, lambda peer: piece_ref.at[0], inbox2, "recv")
        value = inbox2[0]
        for i in range(1, C):
            value = value + inbox2[i]
        piece_ref[1] = value * (1.0 / total)
        row_all(phase + 2, lambda peer: piece_ref.at[1], result, "start")
        result[r] = value * (1.0 / total)

    def finish(phase, piece_ref, result):
        row_all(phase + 2, lambda peer: piece_ref.at[1], result, "recv")
        square = jnp.concatenate([result[i] for i in range(R)], axis=0)
        return square[:rows, :rows]

    def drain(phase, part, inbox, piece_ref, inbox2, result):
        row_all(phase, lambda peer: part.at[peer], inbox, "send")
        col_all(phase + 1, lambda peer: piece_ref.at[0], inbox2, "send")
        if result is not None:
            row_all(phase + 2, lambda peer: piece_ref.at[1], result, "send")

    def small_sum(phase, square, part, inbox, piece_ref, inbox2):
        flat = pack(square)
        part[0] = flat
        row_all(phase, lambda peer: part.at[0], inbox, "start")
        inbox[r] = flat
        row_all(phase, lambda peer: part.at[0], inbox, "recv")
        value = inbox[0]
        for i in range(1, R):
            value = value + inbox[i]
        piece_ref[0] = value
        col_all(phase + 1, lambda peer: piece_ref.at[0], inbox2, "start")
        inbox2[c] = value
        col_all(phase + 1, lambda peer: piece_ref.at[0], inbox2, "recv")
        value = inbox2[0]
        for i in range(1, C):
            value = value + inbox2[i]
        return unpack(value) * (1.0 / total)

    search = search_ref[...]
    stage_square(b_part, contract(search, search, ((1,), (1,))))
    round1(B1, b_part, b_in)

    def lift_target(d, _):
        peer = along_col(d)

        @pl.when(d > 0)
        def _():
            col_copy(TGT, points_ref, tgt_pts.at[peer], peer, peer).wait_recv()

        tgt_lift[:, pl.ds(pl.multiple_of(peer * n, n), n)] = lifted(tgt_pts[peer], rate, False)
        return 0

    lax.fori_loop(0, C, lift_target, 0)
    round2(B1, b_part, b_in, b_piece, b_in2)

    deg[...] = jnp.zeros_like(deg)
    z0 = r // 2
    core0 = lax.rem(r, 2)

    def nearest(i):
        k = i // 2
        half = (k + 1) // 2
        delta = jnp.where(lax.rem(k, 2) == 1, half, Z - half)
        z = lax.rem(z0 + delta, Z)
        return z * 2 + lax.rem(core0 + i, 2)

    def affinities(i, _):
        peer = nearest(i)

        @pl.when(i > 0)
        def _():
            row_copy(SRC, points_ref, src_pts.at[peer], peer, peer).wait_recv()

        sources = lifted(src_pts[peer], rate, True)
        exponent = lax.dot_general(
            sources, tgt_lift[...], (((0,), (0,)), ((), ())), preferred_element_type=jnp.float32
        )
        affinity = jnp.exp2(exponent)
        deg[...] += jnp.sum(affinity.reshape(n // 8, 8, C * n), axis=0)
        tile[pl.ds(pl.multiple_of(peer * n, n), n), :] = affinity.astype(jnp.bfloat16)
        return 0

    lax.fori_loop(0, R, affinities, 0)

    window = lambda peer: deg.at[:, pl.ds(pl.multiple_of(peer * n, n), n)]
    col_all(DEG, window, deg_in, "start")
    deg_in[c] = deg[:, pl.ds(pl.multiple_of(c * n, n), n)]
    round3(B1, b_piece, b_in2, b_res)
    col_all(DEG, window, deg_in, "recv")
    sums = deg_in[0]
    for i in range(1, C):
        sums = sums + deg_in[i]
    degrees = jnp.sum(sums, axis=0, keepdims=True)
    root = lax.rsqrt(degrees)
    root = root * (1.5 - 0.5 * degrees * root * root)
    scal[r] = (search_ref[...] * root).astype(jnp.bfloat16)
    row_all(SCAL, lambda peer: scal.at[r], scal, "start")

    gram_b = finish(B1, b_piece, b_res)
    gram_b_ref[...] = gram_b
    factor = inverse_factor(gram_b[:NEV, :NEV])
    solved = contract(factor, contract(factor, search_ref[:NEV, :], ((1,), (0,))), ((0,), (0,)))

    row_all(SCAL, lambda peer: scal.at[r], scal, "recv")
    pairs = C // 2
    pair0 = c // 2

    def images(j, _):
        pair = lax.rem(pair0 + 1 + j, pairs)
        at = pl.ds(pl.multiple_of(pair * (2 * n), 2 * n), 2 * n)
        value = jnp.dot(scal[0], tile[0:n, at], preferred_element_type=jnp.float32)
        for i in range(1, R):
            value = value + jnp.dot(
                scal[i], tile[i * n : (i + 1) * n, at], preferred_element_type=jnp.float32
            )
        for half in range(2):
            peer = pair * 2 + half
            outp[peer] = value[:, half * n : (half + 1) * n]

            @pl.when(peer != c)
            def _():
                col_copy(OUT, outp.at[peer], out_in.at[c], peer, c).start()

        return 0

    lax.fori_loop(0, pairs, images, 0)
    out_in[c] = outp[c]
    col_all(OUT, lambda peer: outp.at[peer], out_in, "recv")
    sums = out_in[0]
    for i in range(1, C):
        sums = sums + out_in[i]
    applied = sums * root
    applied_ref[...] = applied

    local_a = contract(search_ref[...], applied, ((1,), (1,)))
    stage_square(a_part, local_a)
    round1(A1, a_part, a_in)
    leading = small_sum(X1, local_a[:NEV, :NEV], x_part, x_in, x_piece, x_in2)
    residual = applied[:NEV] - contract(leading, solved, ((0,), (0,)))
    local_r = contract(residual, residual, ((1,), (1,)))
    round2(A1, a_part, a_in, a_piece, a_in2)
    residual_gram = small_sum(Y1, local_r, y_part, y_in, y_piece, y_in2)
    round3(A1, a_piece, a_in2, a_res)
    q_ref[...] = contract(inverse_factor(residual_gram), residual, ((1,), (0,)))
    gram_a_ref[...] = finish(A1, a_piece, a_res)

    col_all(TGT, my_points, tgt_pts, "send")
    row_all(SRC, my_points, src_pts, "send")
    col_all(DEG, window, deg_in, "send")
    row_all(SCAL, lambda peer: scal.at[r], scal, "send")
    col_all(OUT, lambda peer: outp.at[peer], out_in, "send")
    drain(B1, b_part, b_in, b_piece, b_in2, b_res)
    drain(A1, a_part, a_in, a_piece, a_in2, a_res)
    for phase, part, inbox, piece_ref, inbox2 in (
        (X1, x_part, x_in, x_piece, x_in2),
        (Y1, y_part, y_in, y_piece, y_in2),
    ):
        row_all(phase, lambda peer: part.at[0], inbox, "send")
        col_all(phase + 1, lambda peer: piece_ref.at[0], inbox2, "send")


def per_device(R, C, points, search):
    dim, n = points.shape
    rows = search.shape[0]
    f32 = jnp.float32
    piece = LANES // R
    square = lambda: [
        pltpu.VMEM((R, piece, LANES), f32),
        pltpu.VMEM((R, piece, LANES), f32),
        pltpu.VMEM((2, piece, LANES), f32),
        pltpu.VMEM((C, piece, LANES), f32),
        pltpu.VMEM((R, piece, LANES), f32),
    ]
    small = lambda: [
        pltpu.VMEM((1, 8, LANES), f32),
        pltpu.VMEM((R, 8, LANES), f32),
        pltpu.VMEM((1, 8, LANES), f32),
        pltpu.VMEM((C, 8, LANES), f32),
    ]
    vmem = pl.BlockSpec(memory_space=pltpu.VMEM)
    most = max(R, C)
    return pl.pallas_call(
        functools.partial(kernel, R, C, n),
        out_shape=(
            jax.ShapeDtypeStruct((rows, n), f32),
            jax.ShapeDtypeStruct((rows, rows), f32),
            jax.ShapeDtypeStruct((rows, rows), f32),
            jax.ShapeDtypeStruct((NEV, n), f32),
        ),
        in_specs=[vmem, vmem],
        out_specs=(vmem, vmem, vmem, vmem),
        scratch_shapes=[
            pltpu.VMEM((R, dim, n), f32),
            pltpu.VMEM((C, dim, n), f32),
            pltpu.VMEM((DEPTH, C * n), jnp.bfloat16),
            pltpu.VMEM((R * n, C * n), jnp.bfloat16),
            pltpu.VMEM((8, C * n), f32),
            pltpu.VMEM((C, 8, n), f32),
            pltpu.VMEM((R, rows, n), jnp.bfloat16),
            pltpu.VMEM((C, rows, n), f32),
            pltpu.VMEM((C, rows, n), f32),
            *square(),
            *square(),
            *small(),
            *small(),
            pltpu.SemaphoreType.DMA((15, most)),
            pltpu.SemaphoreType.DMA((15, most)),
        ],
        compiler_params=pltpu.CompilerParams(
            collective_id=0, has_side_effects=True, vmem_limit_bytes=60 << 20
        ),
    )(points, search)


def solution(mesh):
    placed = (P(None, ("row", "col")), P(None, ("row", "col")))
    return jax.shard_map(
        functools.partial(per_device, mesh.shape["row"], mesh.shape["col"]),
        mesh=mesh,
        in_specs=placed,
        out_specs=(P(None, ("row", "col")), P(), P(), P(None, ("row", "col"))),
        check_vma=False,
    )
```

time: 712 us -> 127 us (0.18)
  waiting for transfers between devices: 316 us -> 0 us
  blocking collectives: 210 us -> 0 us
  Pallas kernels: 0 us -> 123 us
  matrix products: 115 us -> 0 us
  local copies, waits for them, and re-layouts: 39.2 us -> 3.74 us
  other arithmetic: 15.3 us -> 0 us
  between operations: 14.8 us -> 0.65 us
    psum x1 -> x0, waiting for transfers between devices: 247 us -> none  [per_device(): sum_a, sum_b = lax.psum((local_a, local_b), ('row', 'col'))]
    pallas_call x0 -> x1, Pallas kernels: none -> 123 us  [per_device(): pl.pallas_call(functools.partial(kernel, R, C, n), out_shape=(jax.ShapeDt...]
    dot_general x36 -> x0, matrix products: 114 us -> none  [the longest x16 73.7 us: pair_tile(): lax.dot_general(source_points, target_points, (((0,), (0,)), ((), ())), p...]
    all_gather x3 -> x0, blocking collectives: 78 us -> none  [the longest x1 30.7 us: per_device(): lax.all_gather(scaled, 'row', axis=1, tiled=True)]
    psum x1 -> x0, blocking collectives: 74.3 us -> none  [per_device(): residual_gram = lax.psum(local_r, ('row', 'col')) / point_count]
    reduce_scatter x1 -> x0, waiting for transfers between devices: 69.3 us -> none  [per_device(): lax.psum_scatter(totals, 'col', scatter_dimension=1, tiled=True)]
    unnamed x1 -> x0, blocking collectives: 58.1 us -> none
    dynamic_update_slice x16 -> x0, local copies, waits for them, and re-layouts: 23.6 us -> none  [degree_add_block(): lax.dynamic_update_slice_in_dim(stored, affinity.astype(jnp.bfloat16), of...]
  transfers between devices with their start and end apart: 2 -> 0, of which waited for: 2 -> 0; matrix products, arithmetic and copies ran while one was open for 0% -> 0% of each run, Pallas kernels for 0% -> 0%
where the time goes in v1:
time: 127 us
  Pallas kernels  123 us (97%)
  local copies, waits for them, and re-layouts  3.74 us (3%)
    pallas_call x1, Pallas kernels, per_device(): pl.pallas_call(functools.partial(kernel, R, C, n), out_shape=(jax.ShapeDt...  123 us
    unnamed x10, local copies, waits for them, and re-layouts  3.74 us

profile of v1, /device:TPU:1, one launch (start us, length us, event | category | flops | bytes accessed | tf_op | source)
XLA Modules:
  0.0 127.1 jit_solution(9315491674297550174)
XLA Ops:
  0.6 122.7 %shard_map.57 = (f32[96,256]{1,0:T(8,128)}, f32[96,96]{1,0:T(8,128)}, f32[96,96]{1,0:T(8,128)}, f32[32,256]{1,0:T(8,128)}) custom-call(f32[32,256]{1,0:T(8,128)} %points_ref.1, f32[96,256]{1,0:T(8,128)} %search_ref.1), custom_call_target="tpu_custom_call" | custom-call | tf_op jit(solution)/shard_map/pallas_call | solution.py:369
  123.3 0.0 copy-start.1
  123.3 1.6 %copy.10 = f32[96,256]{1,0:T(8,128)} copy(f32[96,256]{1,0:T(8,128)} %get-tuple-element.8) | data formatting | bytes 196608
  124.9 0.0 copy-done.1
  124.9 0.0 copy-start
  124.9 0.6 copy.11
  125.5 0.2 copy-done
  125.7 0.0 copy-start.2
  125.7 0.6 copy.12
  126.3 0.1 copy-done.2
  126.5 0.6 copy.13
Async XLA Ops:
  123.3 1.6 %copy-start.1 = (f32[96,96]{1,0:T(8,128)S(1)}, f32[96,96]{1,0:T(8,128)}, u32[]{:S(2)}) copy-start(f32[96,96]{1,0:T(8,128)} %get-tuple-element.9) | copy-start | bytes 110596
  124.9 0.8 copy-start
  125.7 0.8 copy-start.2

commit v2 on v1

--- a/solution.py
+++ b/solution.py
@@ -84,15 +84,13 @@
     src_pts, tgt_pts, tgt_lift, tile, deg, deg_in, scal, outp, out_in,
     a_part, a_in, a_piece, a_in2, a_res,
     b_part, b_in, b_piece, b_in2, b_res,
-    x_part, x_in, x_piece, x_in2,
-    y_part, y_in, y_piece, y_in2,
+    x_part, x_in, x_piece, x_in2, image,
     ssem, rsem,
 ):
     r = lax.axis_index("row")
     c = lax.axis_index("col")
     total = R * C * n
     rate = (2.0 / points_ref.shape[0]) * math.log2(math.e)
-    Z = R // 2
 
     def along_row(d):
         return lax.rem(r + d, R)
@@ -112,31 +110,94 @@
             device_id=(r, peer), device_id_type=MESH,
         )
 
-    def row_all(phase, src_of, dst, what):
+    open_ends = {}
+
+    def every(copy, me, size, phase, src_of, dst, what):
         def body(d, _):
-            peer = along_row(d)
+            peer = lax.rem(me + d, size)
             if what == "start":
-                row_copy(phase, src_of(peer), dst.at[r], peer, r).start()
+                copy(phase, src_of(peer), dst.at[me], peer, me).start()
             elif what == "recv":
-                row_copy(phase, src_of(peer), dst.at[peer], peer, peer).wait_recv()
+                copy(phase, src_of(peer), dst.at[peer], peer, peer).wait_recv()
             else:
-                row_copy(phase, src_of(peer), dst.at[r], peer, r).wait_send()
+                copy(phase, src_of(peer), dst.at[me], peer, me).wait_send()
             return 0
 
-        lax.fori_loop(1, R, body, 0)
-
-    def col_all(phase, src_of, dst, what):
-        def body(d, _):
-            peer = along_col(d)
-            if what == "start":
-                col_copy(phase, src_of(peer), dst.at[c], peer, c).start()
-            elif what == "recv":
-                col_copy(phase, src_of(peer), dst.at[peer], peer, peer).wait_recv()
-            else:
-                col_copy(phase, src_of(peer), dst.at[c], peer, c).wait_send()
-            return 0
-
-        lax.fori_loop(1, C, body, 0)
+        if what == "start":
+            for end in ("recv", "send"):
+                open_ends[phase, end] = functools.partial(
+                    every, copy, me, size, phase, src_of, dst, end
+                )
+        else:
+            del open_ends[phase, what]
+        lax.fori_loop(1, size, body, 0)
+
+    row_all = functools.partial(every, row_copy, r, R)
+    col_all = functools.partial(every, col_copy, c, C)
+
+    Z = R // 2
+    z0, core0 = r // 2, lax.rem(r, 2)
+    partner = z0 * 2 + 1 - core0
+
+    def nearest(i):
+        half = (i + 1) // 2
+        return lax.rem(z0 + jnp.where(lax.rem(i, 2) == 1, half, Z - half), Z)
+
+    class Spread:
+        def __init__(self, direct, handed, buffer):
+            self.direct, self.handed, self.buffer = direct, handed, buffer
+
+        def direct_copy(self, src, peer, slot):
+            return row_copy(self.direct, src, self.buffer.at[slot], peer, slot)
+
+        def handed_copy(self, src, slot):
+            return pltpu.make_async_remote_copy(
+                src_ref=src, dst_ref=self.buffer.at[slot], send_sem=ssem.at[self.handed, slot],
+                recv_sem=rsem.at[self.handed, slot], device_id=(partner, c), device_id_type=MESH,
+            )
+
+        def start(self, src):
+            self.src = src
+
+            def body(i, _):
+                self.direct_copy(src, nearest(i) * 2 + core0, r).start()
+                return 0
+
+            self.handed_copy(src, r).start()
+            lax.fori_loop(1, Z, body, 0)
+            open_ends[self.direct, "send"] = self.sent
+
+        def take(self, i):
+            slot = nearest(i) * 2 + core0
+
+            @pl.when(i > 0)
+            def _():
+                self.direct_copy(self.src, slot, slot).wait_recv()
+                self.handed_copy(self.buffer.at[slot], slot).start()
+
+            return slot
+
+        def take_handed(self, i):
+            slot = nearest(i) * 2 + 1 - core0
+            self.handed_copy(self.src, slot).wait_recv()
+            return slot
+
+        def sent(self):
+            def body(i, _):
+                slot = nearest(i) * 2 + core0
+
+                @pl.when(i > 0)
+                def _():
+                    self.direct_copy(self.src, slot, r).wait_send()
+
+                self.handed_copy(self.src, slot).wait_send()
+                return 0
+
+            lax.fori_loop(0, Z, body, 0)
+
+    def drain():
+        for end in list(open_ends.values()):
+            end()
 
     barrier = pltpu.get_barrier_semaphore()
 
@@ -150,14 +211,17 @@
 
     lax.fori_loop(1, R, greet_row, 0)
     lax.fori_loop(1, C, greet_col, 0)
+    search = search_ref[...]
+    local_b = contract(search, search, ((1,), (1,)))
+    src_pts[r] = points_ref[...]
+    tgt_pts[c] = points_ref[...]
     pl.semaphore_wait(barrier, R + C - 2)
 
-    TGT, SRC, DEG, SCAL, OUT, B1, B2, B3, A1, A2, A3, X1, X2, Y1, Y2 = range(15)
+    TGT, SRC, SRC2, DEG, SCAL, SCAL2, OUT, B1, B2, B3, A1, A2, A3, X1, X2 = range(15)
     my_points = lambda peer: points_ref
     col_all(TGT, my_points, tgt_pts, "start")
-    row_all(SRC, my_points, src_pts, "start")
-    src_pts[r] = points_ref[...]
-    tgt_pts[c] = points_ref[...]
+    sources = Spread(SRC, SRC2, src_pts)
+    sources.start(points_ref)
 
     rows = 96
     piece = LANES // R
@@ -199,14 +263,8 @@
         square = jnp.concatenate([result[i] for i in range(R)], axis=0)
         return square[:rows, :rows]
 
-    def drain(phase, part, inbox, piece_ref, inbox2, result):
-        row_all(phase, lambda peer: part.at[peer], inbox, "send")
-        col_all(phase + 1, lambda peer: piece_ref.at[0], inbox2, "send")
-        if result is not None:
-            row_all(phase + 2, lambda peer: piece_ref.at[1], result, "send")
-
-    def small_sum(phase, square, part, inbox, piece_ref, inbox2):
-        flat = pack(square)
+    def small_sum(phase, squares, part, inbox, piece_ref, inbox2):
+        flat = jnp.concatenate([pack(square) for square in squares], axis=0)
         part[0] = flat
         row_all(phase, lambda peer: part.at[0], inbox, "start")
         inbox[r] = flat
@@ -221,10 +279,10 @@
         value = inbox2[0]
         for i in range(1, C):
             value = value + inbox2[i]
-        return unpack(value) * (1.0 / total)
-
-    search = search_ref[...]
-    stage_square(b_part, contract(search, search, ((1,), (1,))))
+        value = value * (1.0 / total)
+        return [unpack(value[8 * i : 8 * i + 8]) for i in range(len(squares))]
+
+    stage_square(b_part, local_b)
     round1(B1, b_part, b_in)
 
     def lift_target(d, _):
@@ -238,36 +296,22 @@
         return 0
 
     lax.fori_loop(0, C, lift_target, 0)
+    del open_ends[TGT, "recv"]
     round2(B1, b_part, b_in, b_piece, b_in2)
 
     deg[...] = jnp.zeros_like(deg)
-    z0 = r // 2
-    core0 = lax.rem(r, 2)
-
-    def nearest(i):
-        k = i // 2
-        half = (k + 1) // 2
-        delta = jnp.where(lax.rem(k, 2) == 1, half, Z - half)
-        z = lax.rem(z0 + delta, Z)
-        return z * 2 + lax.rem(core0 + i, 2)
-
-    def affinities(i, _):
-        peer = nearest(i)
-
-        @pl.when(i > 0)
-        def _():
-            row_copy(SRC, points_ref, src_pts.at[peer], peer, peer).wait_recv()
-
-        sources = lifted(src_pts[peer], rate, True)
+    def affinities(slot):
         exponent = lax.dot_general(
-            sources, tgt_lift[...], (((0,), (0,)), ((), ())), preferred_element_type=jnp.float32
+            lifted(src_pts[slot], rate, True), tgt_lift[...], (((0,), (0,)), ((), ())),
+            preferred_element_type=jnp.float32,
         )
         affinity = jnp.exp2(exponent)
         deg[...] += jnp.sum(affinity.reshape(n // 8, 8, C * n), axis=0)
-        tile[pl.ds(pl.multiple_of(peer * n, n), n), :] = affinity.astype(jnp.bfloat16)
-        return 0
-
-    lax.fori_loop(0, R, affinities, 0)
+        tile[pl.ds(pl.multiple_of(slot * n, n), n), :] = affinity.astype(jnp.bfloat16)
+        return 0
+
+    lax.fori_loop(0, Z, lambda i, _: affinities(sources.take(i)), 0)
+    lax.fori_loop(0, Z, lambda i, _: affinities(sources.take_handed(i)), 0)
 
     window = lambda peer: deg.at[:, pl.ds(pl.multiple_of(peer * n, n), n)]
     col_all(DEG, window, deg_in, "start")
@@ -281,24 +325,50 @@
     root = lax.rsqrt(degrees)
     root = root * (1.5 - 0.5 * degrees * root * root)
     scal[r] = (search_ref[...] * root).astype(jnp.bfloat16)
-    row_all(SCAL, lambda peer: scal.at[r], scal, "start")
+    blocks = Spread(SCAL, SCAL2, scal)
+    blocks.start(scal.at[r])
 
     gram_b = finish(B1, b_piece, b_res)
     gram_b_ref[...] = gram_b
     factor = inverse_factor(gram_b[:NEV, :NEV])
     solved = contract(factor, contract(factor, search_ref[:NEV, :], ((1,), (0,))), ((0,), (0,)))
 
-    row_all(SCAL, lambda peer: scal.at[r], scal, "recv")
+    def near_images(i, _):
+        slot = blocks.take(i)
+        value = jnp.dot(
+            scal[slot], tile[pl.ds(pl.multiple_of(slot * n, n), n), :],
+            preferred_element_type=jnp.float32,
+        )
+
+        @pl.when(i == 0)
+        def _():
+            image[...] = value
+
+        @pl.when(i > 0)
+        def _():
+            image[...] += value
+
+        return 0
+
+    lax.fori_loop(0, Z, near_images, 0)
+
+    def handed_block(i, _):
+        blocks.take_handed(i)
+        return 0
+
+    lax.fori_loop(0, Z, handed_block, 0)
     pairs = C // 2
     pair0 = c // 2
 
     def images(j, _):
         pair = lax.rem(pair0 + 1 + j, pairs)
         at = pl.ds(pl.multiple_of(pair * (2 * n), 2 * n), 2 * n)
-        value = jnp.dot(scal[0], tile[0:n, at], preferred_element_type=jnp.float32)
-        for i in range(1, R):
+        value = image[:, at]
+        for i in range(Z):
+            slot = i * 2 + 1 - core0
             value = value + jnp.dot(
-                scal[i], tile[i * n : (i + 1) * n, at], preferred_element_type=jnp.float32
+                scal[slot], tile[pl.ds(pl.multiple_of(slot * n, n), n), at],
+                preferred_element_type=jnp.float32,
             )
         for half in range(2):
             peer = pair * 2 + half
@@ -311,6 +381,10 @@
         return 0
 
     lax.fori_loop(0, pairs, images, 0)
+    for end in ("recv", "send"):
+        open_ends[OUT, end] = functools.partial(
+            col_all, OUT, lambda peer: outp.at[peer], out_in, end
+        )
     out_in[c] = outp[c]
     col_all(OUT, lambda peer: outp.at[peer], out_in, "recv")
     sums = out_in[0]
@@ -322,28 +396,19 @@
     local_a = contract(search_ref[...], applied, ((1,), (1,)))
     stage_square(a_part, local_a)
     round1(A1, a_part, a_in)
-    leading = small_sum(X1, local_a[:NEV, :NEV], x_part, x_in, x_piece, x_in2)
+    leading, images_gram = small_sum(
+        X1, [local_a[:NEV, :NEV], contract(applied[:NEV], applied[:NEV], ((1,), (1,)))],
+        x_part, x_in, x_piece, x_in2,
+    )
+    round2(A1, a_part, a_in, a_piece, a_in2)
+    projected = contract(factor, leading, ((1,), (0,)))
     residual = applied[:NEV] - contract(leading, solved, ((0,), (0,)))
-    local_r = contract(residual, residual, ((1,), (1,)))
-    round2(A1, a_part, a_in, a_piece, a_in2)
-    residual_gram = small_sum(Y1, local_r, y_part, y_in, y_piece, y_in2)
+    residual_gram = images_gram - contract(projected, projected, ((0,), (0,)))
+    factor_r = inverse_factor(residual_gram)
     round3(A1, a_piece, a_in2, a_res)
-    q_ref[...] = contract(inverse_factor(residual_gram), residual, ((1,), (0,)))
+    q_ref[...] = contract(factor_r, residual, ((1,), (0,)))
     gram_a_ref[...] = finish(A1, a_piece, a_res)
-
-    col_all(TGT, my_points, tgt_pts, "send")
-    row_all(SRC, my_points, src_pts, "send")
-    col_all(DEG, window, deg_in, "send")
-    row_all(SCAL, lambda peer: scal.at[r], scal, "send")
-    col_all(OUT, lambda peer: outp.at[peer], out_in, "send")
-    drain(B1, b_part, b_in, b_piece, b_in2, b_res)
-    drain(A1, a_part, a_in, a_piece, a_in2, a_res)
-    for phase, part, inbox, piece_ref, inbox2 in (
-        (X1, x_part, x_in, x_piece, x_in2),
-        (Y1, y_part, y_in, y_piece, y_in2),
-    ):
-        row_all(phase, lambda peer: part.at[0], inbox, "send")
-        col_all(phase + 1, lambda peer: piece_ref.at[0], inbox2, "send")
+    drain()
 
 
 def per_device(R, C, points, search):
@@ -359,10 +424,10 @@
         pltpu.VMEM((R, piece, LANES), f32),
     ]
     small = lambda: [
-        pltpu.VMEM((1, 8, LANES), f32),
-        pltpu.VMEM((R, 8, LANES), f32),
-        pltpu.VMEM((1, 8, LANES), f32),
-        pltpu.VMEM((C, 8, LANES), f32),
+        pltpu.VMEM((1, 16, LANES), f32),
+        pltpu.VMEM((R, 16, LANES), f32),
+        pltpu.VMEM((1, 16, LANES), f32),
+        pltpu.VMEM((C, 16, LANES), f32),
     ]
     vmem = pl.BlockSpec(memory_space=pltpu.VMEM)
     most = max(R, C)
@@ -389,7 +454,7 @@
             *square(),
             *square(),
             *small(),
-            *small(),
+            pltpu.VMEM((rows, C * n), f32),
             pltpu.SemaphoreType.DMA((15, most)),
             pltpu.SemaphoreType.DMA((15, most)),
         ],

time: 127 us -> 111 us (0.87)
  Pallas kernels: 123 us -> 106 us
    pallas_call x1, Pallas kernels: 123 us -> 106 us  [per_device(): pl.pallas_call(functools.partial(kernel, R, C, n), out_shape=(jax.ShapeDt...]
where the time goes in v2:
time: 111 us
  Pallas kernels  106 us (95%)
  local copies, waits for them, and re-layouts  3.74 us (3%)
    pallas_call x1, Pallas kernels, per_device(): pl.pallas_call(functools.partial(kernel, R, C, n), out_shape=(jax.ShapeDt...  106 us
    unnamed x10, local copies, waits for them, and re-layouts  3.74 us

profile of v2, /device:TPU:1, one launch (start us, length us, event | category | flops | bytes accessed | tf_op | source)
XLA Modules:
  0.0 110.5 jit_solution(13508163093860725859)
XLA Ops:
  0.6 106.1 %shard_map.57 = (f32[96,256]{1,0:T(8,128)}, f32[96,96]{1,0:T(8,128)}, f32[96,96]{1,0:T(8,128)}, f32[32,256]{1,0:T(8,128)}) custom-call(f32[32,256]{1,0:T(8,128)} %points_ref.1, f32[96,256]{1,0:T(8,128)} %search_ref.1), custom_call_target="tpu_custom_call" | custom-call | tf_op jit(solution)/shard_map/pallas_call | solution.py:434
  106.8 0.0 copy-start.1
  106.8 1.6 %copy.10 = f32[96,256]{1,0:T(8,128)} copy(f32[96,256]{1,0:T(8,128)} %get-tuple-element.8) | data formatting | bytes 196608
  108.3 0.0 copy-done.1
  108.3 0.0 copy-start
  108.3 0.6 copy.11
  109.0 0.2 copy-done
  109.2 0.0 copy-start.2
  109.2 0.6 copy.12
  109.8 0.1 copy-done.2
  109.9 0.6 copy.13
Async XLA Ops:
  106.8 1.6 %copy-start.1 = (f32[96,96]{1,0:T(8,128)S(1)}, f32[96,96]{1,0:T(8,128)}, u32[]{:S(2)}) copy-start(f32[96,96]{1,0:T(8,128)} %get-tuple-element.9) | copy-start | bytes 110596
  108.3 0.8 copy-start
  109.2 0.8 copy-start.2

commit v3 on v2

--- a/solution.py
+++ b/solution.py
@@ -13,6 +13,10 @@
 HIGH = lax.Precision.HIGHEST
 DEPTH = 256
 LANES = 128
+
+
+TGT, SRC, SRC2, DEG, SCAL, SCAL2, O1, O2, O3, O4, B1, B2, B3, A1, A2, A3, X1, X2 = range(18)
+PHASES = 18
 
 
 def contract(a, b, dims):
@@ -71,6 +75,13 @@
     return work[:, k : 2 * k] * lax.rsqrt(diagonal)
 
 
+def grid_x(C):
+    size = 1
+    while size * size < C:
+        size *= 2
+    return size
+
+
 def pack(square):
     return jnp.concatenate([square[8 * i : 8 * i + 8, :] for i in range(4)], axis=1)
 
@@ -81,7 +92,8 @@
 
 def kernel(
     R, C, n, points_ref, search_ref, applied_ref, gram_a_ref, gram_b_ref, q_ref,
-    src_pts, tgt_pts, tgt_lift, tile, deg, deg_in, scal, outp, out_in,
+    src_pts, tgt_pts, tgt_lift, tile, deg, deg_in, scal, outp,
+    along_x, along_y, middle_x, middle_y, last_x, last_y,
     a_part, a_in, a_piece, a_in2, a_res,
     b_part, b_in, b_piece, b_in2, b_res,
     x_part, x_in, x_piece, x_in2, image,
@@ -90,6 +102,7 @@
     r = lax.axis_index("row")
     c = lax.axis_index("col")
     total = R * C * n
+    SINGLY = {TGT: C, SRC: R // 2, SRC2: R // 2, SCAL: R // 2}
     rate = (2.0 / points_ref.shape[0]) * math.log2(math.e)
 
     def along_row(d):
@@ -98,29 +111,38 @@
     def along_col(d):
         return lax.rem(c + d, C)
 
+    def arrived(phase, slot):
+        if phase not in SINGLY:
+            return rsem.at[phase]
+        first = PHASES + sum(SINGLY[p] for p in SINGLY if p < phase)
+        return rsem.at[first + slot]
+
     def row_copy(phase, src, dst, peer, slot):
         return pltpu.make_async_remote_copy(
-            src_ref=src, dst_ref=dst, send_sem=ssem.at[phase, peer], recv_sem=rsem.at[phase, slot],
+            src_ref=src, dst_ref=dst, send_sem=ssem.at[phase], recv_sem=arrived(phase, slot),
             device_id=(peer, c), device_id_type=MESH,
         )
 
     def col_copy(phase, src, dst, peer, slot):
         return pltpu.make_async_remote_copy(
-            src_ref=src, dst_ref=dst, send_sem=ssem.at[phase, peer], recv_sem=rsem.at[phase, slot],
+            src_ref=src, dst_ref=dst, send_sem=ssem.at[phase], recv_sem=arrived(phase, slot),
             device_id=(r, peer), device_id_type=MESH,
         )
 
     open_ends = {}
+
+    def await_blocks(copy, phase, buffer, count, what):
+        blocks = buffer.at[pl.ds(0, count)]
+        whole = copy(phase, blocks, blocks, 0, 0)
+        if what == "recv":
+            whole.wait_recv()
+        else:
+            whole.wait_send()
 
     def every(copy, me, size, phase, src_of, dst, what):
         def body(d, _):
             peer = lax.rem(me + d, size)
-            if what == "start":
-                copy(phase, src_of(peer), dst.at[me], peer, me).start()
-            elif what == "recv":
-                copy(phase, src_of(peer), dst.at[peer], peer, peer).wait_recv()
-            else:
-                copy(phase, src_of(peer), dst.at[me], peer, me).wait_send()
+            copy(phase, src_of(peer), dst.at[me], peer, me).start()
             return 0
 
         if what == "start":
@@ -128,9 +150,10 @@
                 open_ends[phase, end] = functools.partial(
                     every, copy, me, size, phase, src_of, dst, end
                 )
+            lax.fori_loop(1, size, body, 0)
         else:
             del open_ends[phase, what]
-        lax.fori_loop(1, size, body, 0)
+            await_blocks(copy, phase, dst, size - 1, what)
 
     row_all = functools.partial(every, row_copy, r, R)
     col_all = functools.partial(every, col_copy, c, C)
@@ -138,6 +161,10 @@
     Z = R // 2
     z0, core0 = r // 2, lax.rem(r, 2)
     partner = z0 * 2 + 1 - core0
+    X = grid_x(C)
+    Y = C // X
+    y, x = c // X, lax.rem(c, X)
+    split = search_ref.shape[0] // 2
 
     def nearest(i):
         half = (i + 1) // 2
@@ -148,12 +175,15 @@
             self.direct, self.handed, self.buffer = direct, handed, buffer
 
         def direct_copy(self, src, peer, slot):
-            return row_copy(self.direct, src, self.buffer.at[slot], peer, slot)
+            return pltpu.make_async_remote_copy(
+                src_ref=src, dst_ref=self.buffer.at[slot], send_sem=ssem.at[self.direct],
+                recv_sem=arrived(self.direct, slot // 2), device_id=(peer, c), device_id_type=MESH,
+            )
 
         def handed_copy(self, src, slot):
             return pltpu.make_async_remote_copy(
-                src_ref=src, dst_ref=self.buffer.at[slot], send_sem=ssem.at[self.handed, slot],
-                recv_sem=rsem.at[self.handed, slot], device_id=(partner, c), device_id_type=MESH,
+                src_ref=src, dst_ref=self.buffer.at[slot], send_sem=ssem.at[self.handed],
+                recv_sem=arrived(self.handed, slot // 2), device_id=(partner, c), device_id_type=MESH,
             )
 
         def start(self, src):
@@ -182,18 +212,12 @@
             self.handed_copy(self.src, slot).wait_recv()
             return slot
 
+        def take_all_handed(self):
+            await_blocks(row_copy, self.handed, self.buffer, Z, "recv")
+
         def sent(self):
-            def body(i, _):
-                slot = nearest(i) * 2 + core0
-
-                @pl.when(i > 0)
-                def _():
-                    self.direct_copy(self.src, slot, r).wait_send()
-
-                self.handed_copy(self.src, slot).wait_send()
-                return 0
-
-            lax.fori_loop(0, Z, body, 0)
+            await_blocks(row_copy, self.direct, self.buffer, Z - 1, "send")
+            await_blocks(row_copy, self.handed, self.buffer, Z, "send")
 
     def drain():
         for end in list(open_ends.values()):
@@ -217,7 +241,6 @@
     tgt_pts[c] = points_ref[...]
     pl.semaphore_wait(barrier, R + C - 2)
 
-    TGT, SRC, SRC2, DEG, SCAL, SCAL2, OUT, B1, B2, B3, A1, A2, A3, X1, X2 = range(15)
     my_points = lambda peer: points_ref
     col_all(TGT, my_points, tgt_pts, "start")
     sources = Spread(SRC, SRC2, src_pts)
@@ -352,11 +375,7 @@
 
     lax.fori_loop(0, Z, near_images, 0)
 
-    def handed_block(i, _):
-        blocks.take_handed(i)
-        return 0
-
-    lax.fori_loop(0, Z, handed_block, 0)
+    blocks.take_all_handed()
     pairs = C // 2
     pair0 = c // 2
 
@@ -371,25 +390,73 @@
                 preferred_element_type=jnp.float32,
             )
         for half in range(2):
-            peer = pair * 2 + half
-            outp[peer] = value[:, half * n : (half + 1) * n]
-
-            @pl.when(peer != c)
-            def _():
-                col_copy(OUT, outp.at[peer], out_in.at[c], peer, c).start()
+            block = pair * 2 + half
+            by, bx = block // X, lax.rem(block, X)
+            mine = value[:, half * n : (half + 1) * n]
+            outp[block, 0] = mine[:split]
+            outp[block, 1] = mine[split:]
+
+            @pl.when(bx != x)
+            def _():
+                col_copy(O1, outp.at[block, 0], along_x.at[x * Y + by], y * X + bx, 0).start()
+
+            @pl.when(bx == x)
+            def _():
+                along_x[x * Y + by] = mine[:split]
+
+            @pl.when(by != y)
+            def _():
+                col_copy(O2, outp.at[block, 1], along_y.at[y * X + bx], by * X + x, 0).start()
+
+            @pl.when(by == y)
+            def _():
+                along_y[y * X + bx] = mine[split:]
 
         return 0
 
     lax.fori_loop(0, pairs, images, 0)
-    for end in ("recv", "send"):
-        open_ends[OUT, end] = functools.partial(
-            col_all, OUT, lambda peer: outp.at[peer], out_in, end
-        )
-    out_in[c] = outp[c]
-    col_all(OUT, lambda peer: outp.at[peer], out_in, "recv")
-    sums = out_in[0]
-    for i in range(1, C):
-        sums = sums + out_in[i]
+
+    def second(phase, inbox, count, size, me, device, middle, last, phase_out):
+        if count > 1:
+            await_blocks(col_copy, phase, inbox, (count - 1) * size, "recv")
+
+        def body(i, _):
+            at = lax.rem(me + 1 + i, size)
+            value = inbox[at]
+            for k in range(1, count):
+                value = value + inbox[k * size + at]
+
+            @pl.when(at != me)
+            def _():
+                middle[at] = value
+                col_copy(phase_out, middle.at[at], last.at[me], device(at), 0).start()
+
+            @pl.when(at == me)
+            def _():
+                last[me] = value
+
+            return 0
+
+        lax.fori_loop(0, size, body, 0)
+
+    second(O1, along_x, X, Y, y, lambda at: at * X + x, middle_y, last_y, O3)
+    second(O2, along_y, Y, X, x, lambda at: y * X + at, middle_x, last_x, O4)
+
+    def ends(what):
+        for phase, buffer, count in (
+            (O1, along_x, (X - 1) * Y), (O2, along_y, (Y - 1) * X), (O3, last_y, Y - 1), (O4, last_x, X - 1),
+        ):
+            if count and not (what == "recv" and phase in (O1, O2)):
+                await_blocks(col_copy, phase, buffer, count, what)
+
+    ends("recv")
+    open_ends[O1, "send"] = functools.partial(ends, "send")
+    upper, lower = last_y[0], last_x[0]
+    for i in range(1, Y):
+        upper = upper + last_y[i]
+    for i in range(1, X):
+        lower = lower + last_x[i]
+    sums = jnp.concatenate([upper, lower], axis=0)
     applied = sums * root
     applied_ref[...] = applied
 
@@ -430,7 +497,8 @@
         pltpu.VMEM((C, 16, LANES), f32),
     ]
     vmem = pl.BlockSpec(memory_space=pltpu.VMEM)
-    most = max(R, C)
+    X = grid_x(C)
+    singly = C + 3 * (R // 2)
     return pl.pallas_call(
         functools.partial(kernel, R, C, n),
         out_shape=(
@@ -449,14 +517,19 @@
             pltpu.VMEM((8, C * n), f32),
             pltpu.VMEM((C, 8, n), f32),
             pltpu.VMEM((R, rows, n), jnp.bfloat16),
-            pltpu.VMEM((C, rows, n), f32),
-            pltpu.VMEM((C, rows, n), f32),
+            pltpu.VMEM((C, 2, rows // 2, n), f32),
+            pltpu.VMEM((C, rows // 2, n), f32),
+            pltpu.VMEM((C, rows // 2, n), f32),
+            pltpu.VMEM((X, rows // 2, n), f32),
+            pltpu.VMEM((C // X, rows // 2, n), f32),
+            pltpu.VMEM((X, rows // 2, n), f32),
+            pltpu.VMEM((C // X, rows // 2, n), f32),
             *square(),
             *square(),
             *small(),
             pltpu.VMEM((rows, C * n), f32),
-            pltpu.SemaphoreType.DMA((15, most)),
-            pltpu.SemaphoreType.DMA((15, most)),
+            pltpu.SemaphoreType.DMA((PHASES,)),
+            pltpu.SemaphoreType.DMA((PHASES + singly,)),
         ],
         compiler_params=pltpu.CompilerParams(
             collective_id=0, has_side_effects=True, vmem_limit_bytes=60 << 20

time: 111 us -> 98.3 us (0.89)
  Pallas kernels: 106 us -> 93.6 us
    pallas_call x1, Pallas kernels: 106 us -> 93.6 us  [per_device(): pl.pallas_call(functools.partial(kernel, R, C, n), out_shape=(jax.ShapeDt...]
where the time goes in v3:
time: 98.3 us; the launch traced here: 98 us
  Pallas kernels  93.6 us (95%)
  local copies, waits for them, and re-layouts  3.74 us (4%)
    pallas_call x1, Pallas kernels, per_device(): pl.pallas_call(functools.partial(kernel, R, C, n), out_shape=(jax.ShapeDt...  93.6 us
    unnamed x10, local copies, waits for them, and re-layouts  3.74 us

profile of v3, /device:TPU:1, one launch (start us, length us, event | category | flops | bytes accessed | tf_op | source)
XLA Modules:
  0.0 98.0 jit_solution(9511622416690392892)
XLA Ops:
  0.6 93.6 %shard_map.57 = (f32[96,256]{1,0:T(8,128)}, f32[96,96]{1,0:T(8,128)}, f32[96,96]{1,0:T(8,128)}, f32[32,256]{1,0:T(8,128)}) custom-call(f32[32,256]{1,0:T(8,128)} %points_ref.1, f32[96,256]{1,0:T(8,128)} %search_ref.1), custom_call_target="tpu_custom_call" | custom-call | tf_op jit(solution)/shard_map/pallas_call | solution.py:502
  94.2 0.0 copy-start.1
  94.3 1.6 %copy.10 = f32[96,256]{1,0:T(8,128)} copy(f32[96,256]{1,0:T(8,128)} %get-tuple-element.8) | data formatting | bytes 196608
  95.8 0.0 copy-done.1
  95.8 0.0 copy-start
  95.8 0.6 copy.11
  96.4 0.2 copy-done
  96.6 0.0 copy-start.2
  96.6 0.6 copy.12
  97.3 0.1 copy-done.2
  97.4 0.6 copy.13
Async XLA Ops:
  94.2 1.6 %copy-start.1 = (f32[96,96]{1,0:T(8,128)S(1)}, f32[96,96]{1,0:T(8,128)}, u32[]{:S(2)}) copy-start(f32[96,96]{1,0:T(8,128)} %get-tuple-element.9) | copy-start | bytes 110596
  95.8 0.8 copy-start
  96.6 0.8 copy-start.2

commit v4 on v3

--- a/solution.py
+++ b/solution.py
@@ -17,6 +17,7 @@
 
 TGT, SRC, SRC2, DEG, SCAL, SCAL2, O1, O2, O3, O4, B1, B2, B3, A1, A2, A3, X1, X2 = range(18)
 PHASES = 18
+NEAR = 3
 
 
 def contract(a, b, dims):
@@ -82,6 +83,19 @@
     return size
 
 
+def nearest_first(X, Y):
+    hops = lambda d, size: min(d, size - d)
+    steps = [(hops(dy, Y) + hops(dx, X), dy * X + dx) for dy in range(Y) for dx in range(X)]
+    return [step for _, step in sorted(steps)]
+
+
+def chosen(i, values):
+    result = values[0]
+    for k, value in enumerate(values):
+        result = jnp.where(i == k, value, result)
+    return result
+
+
 def pack(square):
     return jnp.concatenate([square[8 * i : 8 * i + 8, :] for i in range(4)], axis=1)
 
@@ -96,7 +110,7 @@
     along_x, along_y, middle_x, middle_y, last_x, last_y,
     a_part, a_in, a_piece, a_in2, a_res,
     b_part, b_in, b_piece, b_in2, b_res,
-    x_part, x_in, x_piece, x_in2, image,
+    x_part, x_in, x_piece, x_in2, image, src_lift,
     ssem, rsem,
 ):
     r = lax.axis_index("row")
@@ -165,6 +179,7 @@
     Y = C // X
     y, x = c // X, lax.rem(c, X)
     split = search_ref.shape[0] // 2
+    near = min(NEAR, Z)
 
     def nearest(i):
         half = (i + 1) // 2
@@ -200,10 +215,11 @@
         def take(self, i):
             slot = nearest(i) * 2 + core0
 
-            @pl.when(i > 0)
-            def _():
+            def step():
                 self.direct_copy(self.src, slot, slot).wait_recv()
                 self.handed_copy(self.buffer.at[slot], slot).start()
+
+            step() if isinstance(i, int) else pl.when(i > 0)(step)
 
             return slot
 
@@ -286,55 +302,81 @@
         square = jnp.concatenate([result[i] for i in range(R)], axis=0)
         return square[:rows, :rows]
 
-    def small_sum(phase, squares, part, inbox, piece_ref, inbox2):
+    def small_start(phase, squares, part, inbox):
         flat = jnp.concatenate([pack(square) for square in squares], axis=0)
         part[0] = flat
+        inbox[r] = flat
         row_all(phase, lambda peer: part.at[0], inbox, "start")
-        inbox[r] = flat
+
+    def small_turn(phase, part, inbox, piece_ref, inbox2):
         row_all(phase, lambda peer: part.at[0], inbox, "recv")
         value = inbox[0]
         for i in range(1, R):
             value = value + inbox[i]
         piece_ref[0] = value
+        inbox2[c] = value
         col_all(phase + 1, lambda peer: piece_ref.at[0], inbox2, "start")
-        inbox2[c] = value
+
+    def small_finish(phase, piece_ref, inbox2, count):
         col_all(phase + 1, lambda peer: piece_ref.at[0], inbox2, "recv")
         value = inbox2[0]
         for i in range(1, C):
             value = value + inbox2[i]
         value = value * (1.0 / total)
-        return [unpack(value[8 * i : 8 * i + 8]) for i in range(len(squares))]
+        return [unpack(value[8 * i : 8 * i + 8]) for i in range(count)]
 
     stage_square(b_part, local_b)
     round1(B1, b_part, b_in)
 
-    def lift_target(d, _):
-        peer = along_col(d)
-
-        @pl.when(d > 0)
+    def affinities(exponent, slots, at, width):
+        affinity = jnp.exp2(exponent)
+        rows_in = n * len(slots)
+        deg[:, at] += jnp.sum(affinity.reshape(rows_in // 8, 8, width), axis=0)
+        low = affinity.astype(jnp.bfloat16)
+        for i, slot in enumerate(slots):
+            tile[pl.ds(pl.multiple_of(slot * n, n), n), at] = low[i * n : (i + 1) * n]
+
+    def cross(lifted_sources, lifted_targets):
+        return lax.dot_general(
+            lifted_sources, lifted_targets, (((0,), (0,)), ((), ())),
+            preferred_element_type=jnp.float32,
+        )
+
+    deg[...] = jnp.zeros_like(deg)
+    early = [r, partner]
+    src_lift[:, 0:n] = lifted(points_ref[...], rate, True)
+    sources.take_handed(0)
+    src_lift[:, n : 2 * n] = lifted(src_pts[partner], rate, True)
+    for i in range(1, near):
+        early.append(sources.take(i))
+        src_lift[:, (i + 1) * n : (i + 2) * n] = lifted(src_pts[early[-1]], rate, True)
+
+    def early_cells(i, _):
+        away = chosen(i, nearest_first(X, Y))
+        peer = lax.rem(y + away // X, Y) * X + lax.rem(x + lax.rem(away, X), X)
+
+        @pl.when(i > 0)
         def _():
             col_copy(TGT, points_ref, tgt_pts.at[peer], peer, peer).wait_recv()
 
-        tgt_lift[:, pl.ds(pl.multiple_of(peer * n, n), n)] = lifted(tgt_pts[peer], rate, False)
+        at = pl.ds(pl.multiple_of(peer * n, n), n)
+        targets = lifted(tgt_pts[peer], rate, False)
+        tgt_lift[:, at] = targets
+        affinities(cross(src_lift[...], targets), early, at, n)
         return 0
 
-    lax.fori_loop(0, C, lift_target, 0)
+    lax.fori_loop(0, C, early_cells, 0)
     del open_ends[TGT, "recv"]
     round2(B1, b_part, b_in, b_piece, b_in2)
 
-    deg[...] = jnp.zeros_like(deg)
-    def affinities(slot):
-        exponent = lax.dot_general(
-            lifted(src_pts[slot], rate, True), tgt_lift[...], (((0,), (0,)), ((), ())),
-            preferred_element_type=jnp.float32,
+    def block_row(slot):
+        affinities(
+            cross(lifted(src_pts[slot], rate, True), tgt_lift[...]), [slot], slice(None), C * n
         )
-        affinity = jnp.exp2(exponent)
-        deg[...] += jnp.sum(affinity.reshape(n // 8, 8, C * n), axis=0)
-        tile[pl.ds(pl.multiple_of(slot * n, n), n), :] = affinity.astype(jnp.bfloat16)
         return 0
 
-    lax.fori_loop(0, Z, lambda i, _: affinities(sources.take(i)), 0)
-    lax.fori_loop(0, Z, lambda i, _: affinities(sources.take_handed(i)), 0)
+    lax.fori_loop(near, Z, lambda i, _: block_row(sources.take(i)), 0)
+    lax.fori_loop(1, Z, lambda i, _: block_row(sources.take_handed(i)), 0)
 
     window = lambda peer: deg.at[:, pl.ds(pl.multiple_of(peer * n, n), n)]
     col_all(DEG, window, deg_in, "start")
@@ -460,20 +502,19 @@
     applied = sums * root
     applied_ref[...] = applied
 
-    local_a = contract(search_ref[...], applied, ((1,), (1,)))
-    stage_square(a_part, local_a)
+    leaders = jnp.concatenate([search_ref[:NEV, :], applied[:NEV]], axis=0)
+    products = contract(leaders, applied[:NEV], ((1,), (1,)))
+    small_start(X1, [products[:NEV], products[NEV:]], x_part, x_in)
+    stage_square(a_part, contract(search_ref[...], applied, ((1,), (1,))))
     round1(A1, a_part, a_in)
-    leading, images_gram = small_sum(
-        X1, [local_a[:NEV, :NEV], contract(applied[:NEV], applied[:NEV], ((1,), (1,)))],
-        x_part, x_in, x_piece, x_in2,
-    )
+    small_turn(X1, x_part, x_in, x_piece, x_in2)
     round2(A1, a_part, a_in, a_piece, a_in2)
+    leading, images_gram = small_finish(X1, x_piece, x_in2, 2)
     projected = contract(factor, leading, ((1,), (0,)))
+    residual_gram = images_gram - contract(projected, projected, ((0,), (0,)))
+    round3(A1, a_piece, a_in2, a_res)
     residual = applied[:NEV] - contract(leading, solved, ((0,), (0,)))
-    residual_gram = images_gram - contract(projected, projected, ((0,), (0,)))
-    factor_r = inverse_factor(residual_gram)
-    round3(A1, a_piece, a_in2, a_res)
-    q_ref[...] = contract(factor_r, residual, ((1,), (0,)))
+    q_ref[...] = contract(inverse_factor(residual_gram), residual, ((1,), (0,)))
     gram_a_ref[...] = finish(A1, a_piece, a_res)
     drain()
 
@@ -528,6 +569,7 @@
             *square(),
             *small(),
             pltpu.VMEM((rows, C * n), f32),
+            pltpu.VMEM((DEPTH, (min(NEAR, R // 2) + 1) * n), jnp.bfloat16),
             pltpu.SemaphoreType.DMA((PHASES,)),
             pltpu.SemaphoreType.DMA((PHASES + singly,)),
         ],

time: 98.3 us -> 92.6 us (0.942)
  Pallas kernels: 93.6 us -> 88 us
    pallas_call x1, Pallas kernels: 93.6 us -> 88 us  [per_device(): pl.pallas_call(functools.partial(kernel, R, C, n), out_shape=(jax.ShapeDt...]
where the time goes in v4:
time: 92.6 us; the launch traced here: 92.4 us
  Pallas kernels  88 us (95%)
  local copies, waits for them, and re-layouts  3.74 us (4%)
    pallas_call x1, Pallas kernels, per_device(): pl.pallas_call(functools.partial(kernel, R, C, n), out_shape=(jax.ShapeDt...  88 us
    unnamed x10, local copies, waits for them, and re-layouts  3.74 us

profile of v4, /device:TPU:1, one launch (start us, length us, event | category | flops | bytes accessed | tf_op | source)
XLA Modules:
  0.0 92.4 jit_solution(15332740863999297067)
XLA Ops:
  0.6 88.0 %shard_map.57 = (f32[96,256]{1,0:T(8,128)}, f32[96,96]{1,0:T(8,128)}, f32[96,96]{1,0:T(8,128)}, f32[32,256]{1,0:T(8,128)}) custom-call(f32[32,256]{1,0:T(8,128)} %points_ref.1, f32[96,256]{1,0:T(8,128)} %search_ref.1), custom_call_target="tpu_custom_call" | custom-call | tf_op jit(solution)/shard_map/pallas_call | solution.py:543
  88.6 0.0 copy-start.1
  88.6 1.6 %copy.10 = f32[96,256]{1,0:T(8,128)} copy(f32[96,256]{1,0:T(8,128)} %get-tuple-element.8) | data formatting | bytes 196608
  90.2 0.0 copy-done.1
  90.2 0.0 copy-start
  90.2 0.6 copy.11
  90.8 0.2 copy-done
  91.0 0.0 copy-start.2
  91.0 0.6 copy.12
  91.6 0.1 copy-done.2
  91.7 0.6 copy.13
Async XLA Ops:
  88.6 1.6 %copy-start.1 = (f32[96,96]{1,0:T(8,128)S(1)}, f32[96,96]{1,0:T(8,128)}, u32[]{:S(2)}) copy-start(f32[96,96]{1,0:T(8,128)} %get-tuple-element.9) | copy-start | bytes 110596
  90.2 0.8 copy-start
  91.0 0.8 copy-start.2

commit v5 on v4

--- a/solution.py
+++ b/solution.py
@@ -66,12 +66,22 @@
     eye = jnp.where(row == col, 1.0, 0.0)
     pad = jnp.zeros((k, LANES - 2 * k), jnp.float32)
     work = jnp.concatenate([gram, eye, pad], axis=1)
-    below = lax.broadcasted_iota(jnp.int32, (k, 1), 0)
-    for step in range(k):
-        pivot_row = work[step : step + 1, :]
-        pivot = work[step : step + 1, step : step + 1]
-        factor = jnp.where(below > step, work[:, step : step + 1] / pivot, 0.0)
-        work = work - factor * pivot_row
+    below = lax.broadcasted_iota(jnp.int32, (k, LANES), 0)
+    wide = lambda part, rows: jnp.broadcast_to(part, (rows, LANES))
+    for step in range(0, k, 2):
+        upper, lower = work[step : step + 1, :], work[step + 1 : step + 2, :]
+        first, second = wide(work[:, step : step + 1], k), wide(work[:, step + 1 : step + 2], k)
+        pivot, right = wide(upper[:, step : step + 1], 1), wide(upper[:, step + 1 : step + 2], 1)
+        left, corner = wide(lower[:, step : step + 1], 1), wide(lower[:, step + 1 : step + 2], 1)
+        inverse = 1.0 / pivot
+        ratio = right * inverse
+        upper = upper * inverse
+        lower = (lower - left * upper) * (1.0 / (corner - left * ratio))
+        work = (
+            work
+            - jnp.where(below > step, first, 0.0) * upper
+            - jnp.where(below > step + 1, second - first * ratio, 0.0) * lower
+        )
     diagonal = jnp.sum(work[:, :k] * eye, axis=1, keepdims=True)
     return work[:, k : 2 * k] * lax.rsqrt(diagonal)
 
@@ -110,7 +120,7 @@
     along_x, along_y, middle_x, middle_y, last_x, last_y,
     a_part, a_in, a_piece, a_in2, a_res,
     b_part, b_in, b_piece, b_in2, b_res,
-    x_part, x_in, x_piece, x_in2, image, src_lift,
+    x_part, x_in, x_piece, x_in2, image, src_lift, local_b_ref,
     ssem, rsem,
 ):
     r = lax.axis_index("row")
@@ -252,22 +262,22 @@
     lax.fori_loop(1, R, greet_row, 0)
     lax.fori_loop(1, C, greet_col, 0)
     search = search_ref[...]
-    local_b = contract(search, search, ((1,), (1,)))
+    local_b_ref[...] = contract(search, search, ((1,), (1,)))
     src_pts[r] = points_ref[...]
     tgt_pts[c] = points_ref[...]
     pl.semaphore_wait(barrier, R + C - 2)
 
     my_points = lambda peer: points_ref
-    col_all(TGT, my_points, tgt_pts, "start")
     sources = Spread(SRC, SRC2, src_pts)
     sources.start(points_ref)
+    col_all(TGT, my_points, tgt_pts, "start")
 
     rows = 96
-    piece = LANES // R
+    piece = LANES // C
 
     def stage_square(part, square):
         wide = jnp.concatenate([square, jnp.zeros((rows, LANES - rows), jnp.float32)], axis=1)
-        for i in range(R):
+        for i in range(C):
             if (i + 1) * piece <= rows:
                 part[i] = wide[i * piece : (i + 1) * piece]
             else:
@@ -276,30 +286,30 @@
                 part[i] = jnp.concatenate([wide[i * piece : i * piece + live], rest], axis=0) if live else rest
 
     def round1(phase, part, inbox):
-        row_all(phase, lambda peer: part.at[peer], inbox, "start")
-        inbox[r] = part[r]
+        col_all(phase, lambda peer: part.at[peer], inbox, "start")
+        inbox[c] = part[c]
 
     def round2(phase, part, inbox, piece_ref, inbox2):
-        row_all(phase, lambda peer: part.at[peer], inbox, "recv")
+        col_all(phase, lambda peer: part.at[peer], inbox, "recv")
         value = inbox[0]
-        for i in range(1, R):
+        for i in range(1, C):
             value = value + inbox[i]
         piece_ref[0] = value
-        col_all(phase + 1, lambda peer: piece_ref.at[0], inbox2, "start")
-        inbox2[c] = value
+        row_all(phase + 1, lambda peer: piece_ref.at[0], inbox2, "start")
+        inbox2[r] = value
 
     def round3(phase, piece_ref, inbox2, result):
-        col_all(phase + 1, lambda peer: piece_ref.at[0], inbox2, "recv")
+        row_all(phase + 1, lambda peer: piece_ref.at[0], inbox2, "recv")
         value = inbox2[0]
-        for i in range(1, C):
+        for i in range(1, R):
             value = value + inbox2[i]
         piece_ref[1] = value * (1.0 / total)
-        row_all(phase + 2, lambda peer: piece_ref.at[1], result, "start")
-        result[r] = value * (1.0 / total)
+        col_all(phase + 2, lambda peer: piece_ref.at[1], result, "start")
+        result[c] = value * (1.0 / total)
 
     def finish(phase, piece_ref, result):
-        row_all(phase + 2, lambda peer: piece_ref.at[1], result, "recv")
-        square = jnp.concatenate([result[i] for i in range(R)], axis=0)
+        col_all(phase + 2, lambda peer: piece_ref.at[1], result, "recv")
+        square = jnp.concatenate([result[i] for i in range(C)], axis=0)
         return square[:rows, :rows]
 
     def small_start(phase, squares, part, inbox):
@@ -325,8 +335,6 @@
         value = value * (1.0 / total)
         return [unpack(value[8 * i : 8 * i + 8]) for i in range(count)]
 
-    stage_square(b_part, local_b)
-    round1(B1, b_part, b_in)
 
     def affinities(exponent, slots, at, width):
         affinity = jnp.exp2(exponent)
@@ -367,21 +375,25 @@
 
     lax.fori_loop(0, C, early_cells, 0)
     del open_ends[TGT, "recv"]
-    round2(B1, b_part, b_in, b_piece, b_in2)
-
-    def block_row(slot):
+    stage_square(b_part, local_b_ref[...])
+    round1(B1, b_part, b_in)
+
+    def block_rows(slots):
+        lifts = [lifted(src_pts[slot], rate, True) for slot in slots]
         affinities(
-            cross(lifted(src_pts[slot], rate, True), tgt_lift[...]), [slot], slice(None), C * n
+            cross(jnp.concatenate(lifts, axis=1), tgt_lift[...]), slots, slice(None), C * n
         )
         return 0
 
-    lax.fori_loop(near, Z, lambda i, _: block_row(sources.take(i)), 0)
-    lax.fori_loop(1, Z, lambda i, _: block_row(sources.take_handed(i)), 0)
+    lax.fori_loop(
+        near, Z, lambda i, _: block_rows([sources.take(i), sources.take_handed(i - near + 1)]), 0
+    )
+    block_rows([sources.take_handed(i) for i in range(Z - near + 1, Z)])
 
     window = lambda peer: deg.at[:, pl.ds(pl.multiple_of(peer * n, n), n)]
     col_all(DEG, window, deg_in, "start")
     deg_in[c] = deg[:, pl.ds(pl.multiple_of(c * n, n), n)]
-    round3(B1, b_piece, b_in2, b_res)
+    round2(B1, b_part, b_in, b_piece, b_in2)
     col_all(DEG, window, deg_in, "recv")
     sums = deg_in[0]
     for i in range(1, C):
@@ -393,11 +405,6 @@
     blocks = Spread(SCAL, SCAL2, scal)
     blocks.start(scal.at[r])
 
-    gram_b = finish(B1, b_piece, b_res)
-    gram_b_ref[...] = gram_b
-    factor = inverse_factor(gram_b[:NEV, :NEV])
-    solved = contract(factor, contract(factor, search_ref[:NEV, :], ((1,), (0,))), ((0,), (0,)))
-
     def near_images(i, _):
         slot = blocks.take(i)
         value = jnp.dot(
@@ -417,6 +424,7 @@
 
     lax.fori_loop(0, Z, near_images, 0)
 
+    round3(B1, b_piece, b_in2, b_res)
     blocks.take_all_handed()
     pairs = C // 2
     pair0 = c // 2
@@ -481,6 +489,10 @@
 
         lax.fori_loop(0, size, body, 0)
 
+    gram_b = finish(B1, b_piece, b_res)
+    gram_b_ref[...] = gram_b
+    factor = inverse_factor(gram_b[:NEV, :NEV])
+
     second(O1, along_x, X, Y, y, lambda at: at * X + x, middle_y, last_y, O3)
     second(O2, along_y, Y, X, x, lambda at: y * X + at, middle_x, last_x, O4)
 
@@ -502,13 +514,14 @@
     applied = sums * root
     applied_ref[...] = applied
 
-    leaders = jnp.concatenate([search_ref[:NEV, :], applied[:NEV]], axis=0)
-    products = contract(leaders, applied[:NEV], ((1,), (1,)))
-    small_start(X1, [products[:NEV], products[NEV:]], x_part, x_in)
-    stage_square(a_part, contract(search_ref[...], applied, ((1,), (1,))))
+    both = jnp.concatenate([search_ref[...], applied[:NEV]], axis=0)
+    products = contract(both, applied, ((1,), (1,)))
+    small_start(X1, [products[:NEV, :NEV], products[rows:, :NEV]], x_part, x_in)
+    stage_square(a_part, products[:rows])
     round1(A1, a_part, a_in)
     small_turn(X1, x_part, x_in, x_piece, x_in2)
     round2(A1, a_part, a_in, a_piece, a_in2)
+    solved = contract(factor, contract(factor, search_ref[:NEV, :], ((1,), (0,))), ((0,), (0,)))
     leading, images_gram = small_finish(X1, x_piece, x_in2, 2)
     projected = contract(factor, leading, ((1,), (0,)))
     residual_gram = images_gram - contract(projected, projected, ((0,), (0,)))
@@ -523,13 +536,13 @@
     dim, n = points.shape
     rows = search.shape[0]
     f32 = jnp.float32
-    piece = LANES // R
+    piece = LANES // C
     square = lambda: [
+        pltpu.VMEM((C, piece, LANES), f32),
+        pltpu.VMEM((C, piece, LANES), f32),
+        pltpu.VMEM((2, piece, LANES), f32),
         pltpu.VMEM((R, piece, LANES), f32),
-        pltpu.VMEM((R, piece, LANES), f32),
-        pltpu.VMEM((2, piece, LANES), f32),
         pltpu.VMEM((C, piece, LANES), f32),
-        pltpu.VMEM((R, piece, LANES), f32),
     ]
     small = lambda: [
         pltpu.VMEM((1, 16, LANES), f32),
@@ -570,6 +583,7 @@
             *small(),
             pltpu.VMEM((rows, C * n), f32),
             pltpu.VMEM((DEPTH, (min(NEAR, R // 2) + 1) * n), jnp.bfloat16),
+            pltpu.VMEM((rows, rows), f32),
             pltpu.SemaphoreType.DMA((PHASES,)),
             pltpu.SemaphoreType.DMA((PHASES + singly,)),
         ],

time: 92.6 us -> 90.6 us (0.978)
  Pallas kernels: 88 us -> 85.9 us
    pallas_call x1, Pallas kernels: 88 us -> 85.9 us  [per_device(): pl.pallas_call(functools.partial(kernel, R, C, n), out_shape=(jax.ShapeDt...]
where the time goes in v5:
time: 90.6 us; the launch traced here: 90.3 us
  Pallas kernels  85.9 us (95%)
  local copies, waits for them, and re-layouts  3.74 us (4%)
    pallas_call x1, Pallas kernels, per_device(): pl.pallas_call(functools.partial(kernel, R, C, n), out_shape=(jax.ShapeDt...  85.9 us
    unnamed x10, local copies, waits for them, and re-layouts  3.74 us

profile of v5, /device:TPU:1, one launch (start us, length us, event | category | flops | bytes accessed | tf_op | source)
XLA Modules:
  0.0 90.3 jit_solution(9329170219611915146)
XLA Ops:
  0.6 85.9 %shard_map.57 = (f32[96,256]{1,0:T(8,128)}, f32[96,96]{1,0:T(8,128)}, f32[96,96]{1,0:T(8,128)}, f32[32,256]{1,0:T(8,128)}) custom-call(f32[32,256]{1,0:T(8,128)} %points_ref.1, f32[96,256]{1,0:T(8,128)} %search_ref.1), custom_call_target="tpu_custom_call" | custom-call | tf_op jit(solution)/shard_map/pallas_call | solution.py:556
  86.5 0.0 copy-start.1
  86.5 1.6 %copy.10 = f32[96,256]{1,0:T(8,128)} copy(f32[96,256]{1,0:T(8,128)} %get-tuple-element.8) | data formatting | bytes 196608
  88.1 0.0 copy-done.1
  88.1 0.0 copy-start
  88.1 0.6 copy.11
  88.7 0.2 copy-done
  88.9 0.0 copy-start.2
  88.9 0.6 copy.12
  89.5 0.1 copy-done.2
  89.7 0.6 copy.13
Async XLA Ops:
  86.5 1.6 %copy-start.1 = (f32[96,96]{1,0:T(8,128)S(1)}, f32[96,96]{1,0:T(8,128)}, u32[]{:S(2)}) copy-start(f32[96,96]{1,0:T(8,128)} %get-tuple-element.9) | copy-start | bytes 110596
  88.1 0.8 copy-start
  88.9 0.8 copy-start.2
